TPU v7x, 32 devices: a whole 2x2x4 slice. The times are simulated.
32 devices in a mesh: region: 4 (over z), member: 8 (over y, x, core).
Axes of the slice: x: 2, y: 2, z: 4, core: 2. Of those that a mesh axis runs over, the one named last changes fastest.
Arguments:
- ensemble: float32 [256, 1024], P('member', 'region'), may hold values from -6 to 6
- obs_value: float32 [2048], replicated, may hold values from -6 to 6
- obs_error: float32 [2048], replicated, may hold values from 0.5 to 2
- obs_region: int32 [2048], replicated, may hold values from 0 to 3
- obs_cell: int32 [2048], replicated, may hold values from 0 to 255
- order: int32 [2048], replicated, may hold values from 0 to 2047, each once
- footprint: int32 [2, 8, 2], P(None, 'region'), may hold values from 0 to 15, as said below
Outputs:
- analysis: float32 [256, 1024], P('member', 'region')
Inputs may be any that keep to these rules, and one draw needn't show every extreme that they name: `footprint`: the 2 observation tiles listed for one state tile and batch are different.
All inputs are finite; a program needn't handle non-finite values.
Results may differ from a plain program's by a relative error of at most 0.0003.
Values sent between devices are 32-bit elements; how exact they have to be, the bound alone decides.
A program may use at most 64 MiB of HBM per device.

v0:
```python
import jax
import jax.numpy as jnp
from jax import lax
from jax.sharding import PartitionSpec as P

NOBS = 1024
BATCHES = 2
STILE = 128
OTILE = 64
FOOT = 2


def per_device(ensemble, obs_value, obs_error, obs_region, obs_cell, order, footprint):
    mem_dev, cell_count = ensemble.shape
    members = mem_dev * lax.axis_size("member")
    tile_count = cell_count // STILE
    state = ensemble
    region = lax.axis_index("region")
    offsets = jnp.arange(OTILE, dtype=jnp.int32)
    for batch_no in range(BATCHES):
        chosen = order[batch_no * NOBS : (batch_no + 1) * NOBS]
        owned_here = obs_region[chosen] == region
        picked = jnp.where(owned_here[None, :], jnp.take(state, obs_cell[chosen], axis=1), 0.0)
        priors = lax.psum(picked, "region")
        obs_index = (footprint[batch_no][:, :, None] * OTILE + offsets[None, None, :]).reshape(
            tile_count, FOOT * OTILE
        )
        state_tiles = state.reshape(mem_dev, tile_count, STILE)
        s_one = jnp.sum(priors, axis=0)
        s_two = jnp.sum(priors * priors, axis=0)
        s_one, s_two = lax.psum((s_one, s_two), "member")
        obs_mean = s_one / members
        obs_pert = priors - obs_mean[None, :]
        obs_tiles = jnp.take(obs_pert, obs_index, axis=1)
        partial_value = jnp.einsum(
            "mtj,mtc->tjc", obs_tiles, state_tiles, precision=lax.Precision.HIGHEST
        )
        summed = lax.psum(partial_value, "member")
        covariance = summed / (members - 1)
        obs_var = (s_two - s_one * obs_mean) / (members - 1)
        err_var = obs_error[chosen]
        obs_gain = 1.0 / (obs_var + err_var)
        shrink = 1.0 / (1.0 + jnp.sqrt(err_var * obs_gain))
        innovation = obs_value[chosen] - obs_mean
        weight = covariance * obs_gain[obs_index][:, :, None]
        mean_step = jnp.einsum(
            "tjc,tj->tc", weight, innovation[obs_index], precision=lax.Precision.HIGHEST
        )
        scaled = obs_tiles * shrink[obs_index][None, :, :]
        pert_step = jnp.einsum("mtj,tjc->mtc", scaled, weight, precision=lax.Precision.HIGHEST)
        state = (
            state + mean_step.reshape(cell_count)[None, :] - pert_step.reshape(mem_dev, cell_count)
        )
    return state


def solution(mesh):
    in_specs = (P("member", "region"), P(), P(), P(), P(), P(), P(None, "region", None))
    out_specs = P("member", "region")
    return jax.shard_map(
        per_device, mesh=mesh, in_specs=in_specs, out_specs=out_specs, check_vma=False
    )
```

profile of v0, /device:TPU:0, one launch (start us, length us, event | category | flops | bytes accessed | tf_op | source)
XLA Modules:
  0.0 252.9 jit_solution(2424373004848491540)
XLA Ops:
  6.5 0.7 fusion.33
  7.3 6.2 %gather_fusion.1 = s32[1024]{0:T(1024)S(1)} fusion(s32[2048]{0:T(1024)S(1)} %copy-done, s32[1024]{0:T(1024)S(1)} %get-tuple-element.20), kind=kCustom, calls=%fused_computation.5 | custom fusion | bytes 12288 | tf_op jit(solution)/shard_map/gather | solution.py:23
  13.4 6.2 %gather_fusion = s32[1024]{0:T(1024)S(1)} fusion(s32[2048]{0:T(1024)S(1)} %copy-done.1, s32[1024]{0:T(1024)S(1)} %get-tuple-element.20), kind=kCustom, calls=%fused_computation.4 | custom fusion | bytes 12288 | tf_op jit(solution)/shard_map/gather | solution.py:22
  19.6 0.1 copy.26
  19.8 2.8 %gather_fusion.14 = f32[1024,32]{1,0:T(8,128)S(1)} fusion(f32[32,256]{0,1:T(8,128)S(1)} %copy.26, s32[1024]{0:T(1024)S(1)} %fusion.34), kind=kCustom, calls=%fused_computation.clone | custom fusion | bytes 266240 | tf_op jit(solution)/shard_map/jit(_take)/gather | solution.py:23
  22.6 1.1 bitcast_select_fusion.1
  23.8 0.6 copy-done.9
  24.5 0.1 add.172
  24.6 0.1 add.188
  24.7 0.1 add.174
  24.8 0.1 add.178
  24.9 0.1 add.191
  25.0 6.1 %gather_fusion.8 = s32[1024]{0:T(1024)S(1)} fusion(s32[2048]{0:T(1024)S(1)} %copy-done, s32[1024]{0:T(1024)S(1)} %get-tuple-element.19), kind=kCustom, calls=%fused_computation.12 | custom fusion | bytes 12288 | tf_op jit(solution)/shard_map/gather | solution.py:23
  31.1 6.2 %gather_fusion.7 = s32[1024]{0:T(1024)S(1)} fusion(s32[2048]{0:T(1024)S(1)} %copy-done.1, s32[1024]{0:T(1024)S(1)} %get-tuple-element.19), kind=kCustom, calls=%fused_computation.11 | custom fusion | bytes 12288 | tf_op jit(solution)/shard_map/gather | solution.py:22
  37.4 0.7 copy-done.2
  38.0 6.1 %gather_fusion.2 = f32[1024]{0:T(1024)S(1)} fusion(f32[2048]{0:T(1024)S(1)} %copy-done.2, s32[1024]{0:T(1024)S(1)} %get-tuple-element.20), kind=kCustom, calls=%fused_computation.6 | custom fusion | bytes 12288 | tf_op jit(solution)/shard_map/gather | solution.py:41
  44.2 6.2 %gather_fusion.4 = f32[1024]{0:T(1024)S(1)} fusion(f32[2048]{0:T(1024)S(1)} %copy-done.3, s32[1024]{0:T(1024)S(1)} %get-tuple-element.20), kind=kCustom, calls=%fused_computation.8 | custom fusion | bytes 12288 | tf_op jit(solution)/shard_map/gather | solution.py:44
  50.4 14.5 %all-reduce.7.cloned.1.call-done = f32[32,1024]{0,1:T(8,128)} async-done(((f32[32,1024]{0,1:T(8,128)}), f32[32,1024]{0,1:T(8,128)}) %all-reduce.7.cloned.1.call-update) | async-done | bytes 131088 | tf_op jit(solution)/shard_map/psum | solution.py:24
  64.9 1.4 multiply_reduce_fusion.1
  66.3 13.2 %all-reduce.1 = (f32[1024]{0:T(1024)S(1)}, f32[1024]{0:T(1024)S(1)}) all-reduce(f32[1024]{0:T(1024)S(1)} %get-tuple-element.10, f32[1024]{0:T(1024)S(1)} %get-tuple-element.9), channel_id=1, replica_groups=mesh['region'=4,'member'=8] {'member'}, use_global_device_ids=true, to_apply=%region_2.4 | all-reduce | flops 2048 | bytes 16384 | tf_op jit(solution)/shard_map/psum | solution.py:31
  79.5 0.2 broadcast_subtract_fusion.1
  79.7 0.7 gather_fusion.15
  80.6 1.0 fusion.13
  81.7 1.4 gather_fusion.3
  83.1 1.4 gather_fusion.5
  84.4 1.4 gather_fusion.6
  85.8 46.9 %all-reduce.9.cloned.1.call-done = f32[2,128,128]{2,1,0:T(8,128)} async-done(((f32[2,128,128]{2,1,0:T(8,128)}), f32[2,128,128]{2,1,0:T(8,128)}) %all-reduce.9.cloned.1.call-update) | async-done | bytes 131088 | tf_op jit(solution)/shard_map/psum | solution.py:38
  132.7 1.3 fusion.4
  134.0 0.3 convolution_bitcast_fusion.1
  134.3 0.1 copy.30
  134.4 2.8 %gather_fusion.16 = f32[1024,32]{1,0:T(8,128)S(1)} fusion(f32[32,256]{0,1:T(8,128)S(1)} %copy.30, s32[1024]{0:T(1024)S(1)} %fusion.35), kind=kCustom, calls=%fused_computation.2.clone | custom fusion | bytes 266240 | tf_op jit(solution)/shard_map/jit(_take)/gather | solution.py:23
  137.3 1.1 bitcast_select_fusion
  138.5 6.2 %gather_fusion.9 = f32[1024]{0:T(1024)S(1)} fusion(f32[2048]{0:T(1024)S(1)} %copy-done.2, s32[1024]{0:T(1024)S(1)} %get-tuple-element.19), kind=kCustom, calls=%fused_computation.13 | custom fusion | bytes 12288 | tf_op jit(solution)/shard_map/gather | solution.py:41
  144.6 6.2 %gather_fusion.11 = f32[1024]{0:T(1024)S(1)} fusion(f32[2048]{0:T(1024)S(1)} %copy-done.3, s32[1024]{0:T(1024)S(1)} %get-tuple-element.19), kind=kCustom, calls=%fused_computation.15 | custom fusion | bytes 12288 | tf_op jit(solution)/shard_map/gather | solution.py:44
  150.8 25.4 %all-reduce.11.cloned.1.call-done = f32[32,1024]{0,1:T(8,128)} async-done(((f32[32,1024]{0,1:T(8,128)}), f32[32,1024]{0,1:T(8,128)}) %all-reduce.11.cloned.1.call-update) | async-done | bytes 131088 | tf_op jit(solution)/shard_map/psum | solution.py:24
  176.2 1.4 multiply_reduce_fusion
  177.7 13.2 %all-reduce = (f32[1024]{0:T(1024)S(1)}, f32[1024]{0:T(1024)S(1)}) all-reduce(f32[1024]{0:T(1024)S(1)} %get-tuple-element.8, f32[1024]{0:T(1024)S(1)} %get-tuple-element.6), channel_id=1, replica_groups=mesh['region'=4,'member'=8] {'member'}, use_global_device_ids=true, to_apply=%region_8.11 | all-reduce | flops 2048 | bytes 16384 | tf_op jit(solution)/shard_map/psum | solution.py:31
  190.9 0.2 broadcast_subtract_fusion
  191.1 0.7 gather_fusion.17
  191.9 0.1 copy.31
  191.9 1.0 fusion.10
  193.0 1.4 gather_fusion.10
  194.4 1.4 gather_fusion.12
  195.8 1.4 gather_fusion.13
  197.1 47.0 %all-reduce.13.cloned.1.call-done = f32[2,128,128]{2,1,0:T(8,128)} async-done(((f32[2,128,128]{2,1,0:T(8,128)}), f32[2,128,128]{2,1,0:T(8,128)}) %all-reduce.13.cloned.1.call-update) | async-done | bytes 131088 | tf_op jit(solution)/shard_map/psum | solution.py:38
  244.1 1.3 fusion.1
  245.4 0.3 convolution_bitcast_fusion
  245.7 0.6 bitcast_subtract_fusion
  (46 shorter events, 0.6 us)
Async XLA Ops:
  6.5 0.7 copy-start
  6.5 58.3 %all-reduce.7.cloned.1.call-start = ((), (), s32[]{:S(2)}) async-start(), calls=%async_computation | async-start | bytes 1048576 | tf_op jit(solution)/shard_map/psum | solution.py:24
  7.3 6.2 %copy-start.1 = (s32[2048]{0:T(1024)S(1)}, s32[2048]{0:T(1024)}, u32[]{:S(2)}) copy-start(s32[2048]{0:T(1024)} %param.14) | copy-start | bytes 24580
  13.4 6.2 %copy-start.8 = (f32[32,256]{1,0:T(8,128)S(1)}, f32[32,256]{1,0:T(8,128)}, u32[]{:S(2)}) copy-start(f32[32,256]{1,0:T(8,128)} %param.11) | copy-start | bytes 98308
  23.7 0.7 copy-start.9
  23.7 109.0 %all-reduce.9.cloned.1.call-start = ((), (), s32[]{:S(2)}) async-start(), calls=%async_computation.1 | async-start | bytes 262144 | tf_op jit(solution)/shard_map/psum | solution.py:38
  37.3 0.7 copy-start.2
  38.0 6.2 %copy-start.3 = (f32[2048]{0:T(1024)S(1)}, f32[2048]{0:T(1024)}, u32[]{:S(2)}) copy-start(f32[2048]{0:T(1024)} %param.12) | copy-start | bytes 24580
  64.9 14.7 %copy-start.4 = (f32[32,1024]{0,1:T(8,128)S(1)}, f32[32,1024]{0,1:T(8,128)}, u32[]{:S(2)}) copy-start(f32[32,1024]{0,1:T(8,128)} %all-reduce.7.cloned.1.call-done) | copy-start | bytes 393220
  81.6 94.6 %all-reduce.11.cloned.1.call-start = ((), (), s32[]{:S(2)}) async-start(), calls=%async_computation.2 | async-start | bytes 1048576 | tf_op jit(solution)/shard_map/psum | solution.py:24
  132.7 1.3 copy-start.6
  138.4 105.7 %all-reduce.13.cloned.1.call-start = ((), (), s32[]{:S(2)}) async-start(), calls=%async_computation.3 | async-start | bytes 262144 | tf_op jit(solution)/shard_map/psum | solution.py:38
  176.2 14.7 %copy-start.5 = (f32[32,1024]{0,1:T(8,128)S(1)}, f32[32,1024]{0,1:T(8,128)}, u32[]{:S(2)}) copy-start(f32[32,1024]{0,1:T(8,128)} %all-reduce.11.cloned.1.call-done) | copy-start | bytes 393220
  244.1 1.3 copy-start.7
Sparse Core Ops, SparseCore 0:
  23.9 40.9 all-reduce.6
  81.7 50.9 all-reduce.8
  138.6 37.6 all-reduce.10
  193.1 50.9 all-reduce.12
where the time goes:
time: 253 us
  waiting for transfers between devices  134 us (53%)
  local copies, waits for them, and re-layouts  66.7 us (26%)
  blocking collectives  26.3 us (10%)
  between operations  13.5 us (5%)
  other arithmetic  7.04 us (3%)
  matrix products  5.26 us (2%)
    psum x2, waiting for transfers between devices, per_device(): summed = lax.psum(partial_value, 'member')  93.9 us
    psum x2, waiting for transfers between devices, per_device(): priors = lax.psum(picked, 'region')  39.9 us
    psum x2, blocking collectives, per_device(): s_one, s_two = lax.psum((s_one, s_two), 'member')  26.3 us
    gather x2, local copies, waits for them, and re-layouts, per_device(): owned_here = obs_region[chosen] == region  12.3 us
    gather x2, local copies, waits for them, and re-layouts, per_device(): innovation = obs_value[chosen] - obs_mean  12.3 us
    gather x2, local copies, waits for them, and re-layouts, per_device(): obs_cell[chosen]  12.3 us
    gather x2, local copies, waits for them, and re-layouts, per_device(): err_var = obs_error[chosen]  12.3 us
    gather x2, local copies, waits for them, and re-layouts, per_device(): jnp.take(state, obs_cell[chosen], axis=1)  5.64 us
  transfers between devices with their start and end apart: 4, of which 4 were waited for; matrix products, arithmetic and copies ran while one was open for 18% of the time, Pallas kernels for 0%

commit v1 on v0

--- a/solution.py
+++ b/solution.py
@@ -35,7 +35,7 @@
         partial_value = jnp.einsum(
             "mtj,mtc->tjc", obs_tiles, state_tiles, precision=lax.Precision.HIGHEST
         )
-        summed = lax.psum(partial_value, "member")
+        summed = jnp.sum(lax.all_gather(partial_value, "member"), axis=0)
         covariance = summed / (members - 1)
         obs_var = (s_two - s_one * obs_mean) / (members - 1)
         err_var = obs_error[chosen]

time: 253 us -> 196 us (0.77)
  waiting for transfers between devices: 134 us -> 75.9 us
  other arithmetic: 7.04 us -> 9.64 us
    psum x2 -> x0, waiting for transfers between devices: 93.9 us -> none  [per_device(): summed = lax.psum(partial_value, 'member')]
    all_gather x0 -> x2, waiting for transfers between devices: none -> 22.5 us  [per_device(): summed = jnp.sum(lax.all_gather(partial_value, 'member'), axis=0)]
    psum x2, waiting for transfers between devices: 39.9 us -> 53.3 us  [per_device(): priors = lax.psum(picked, 'region')]
    reduce_sum x0 -> x2, other arithmetic: none -> 2.59 us  [per_device(): summed = jnp.sum(lax.all_gather(partial_value, 'member'), axis=0)]
  transfers between devices with their start and end apart: 4 -> 4, of which waited for: 4 -> 4; matrix products, arithmetic and copies ran while one was open for 18% -> 23% of each run, Pallas kernels for 0% -> 0%
where the time goes in v1:
time: 196 us
  waiting for transfers between devices  75.9 us (39%)
  local copies, waits for them, and re-layouts  67.1 us (34%)
  blocking collectives  26.3 us (13%)
  between operations  13.5 us (7%)
  other arithmetic  9.64 us (5%)
  matrix products  3.34 us (2%)
    psum x2, waiting for transfers between devices, per_device(): priors = lax.psum(picked, 'region')  53.3 us
    psum x2, blocking collectives, per_device(): s_one, s_two = lax.psum((s_one, s_two), 'member')  26.3 us
    all_gather x2, waiting for transfers between devices, per_device(): summed = jnp.sum(lax.all_gather(partial_value, 'member'), axis=0)  22.5 us
    gather x2, local copies, waits for them, and re-layouts, per_device(): err_var = obs_error[chosen]  12.3 us
    gather x2, local copies, waits for them, and re-layouts, per_device(): owned_here = obs_region[chosen] == region  12.3 us
    gather x2, local copies, waits for them, and re-layouts, per_device(): innovation = obs_value[chosen] - obs_mean  12.3 us
    gather x2, local copies, waits for them, and re-layouts, per_device(): obs_cell[chosen]  12.3 us
    gather x2, local copies, waits for them, and re-layouts, per_device(): jnp.take(state, obs_cell[chosen], axis=1)  5.64 us
  transfers between devices with their start and end apart: 4, of which 4 were waited for; matrix products, arithmetic and copies ran while one was open for 23% of the time, Pallas kernels for 0%

profile of v1, /device:TPU:0, one launch (start us, length us, event | category | flops | bytes accessed | tf_op | source)
XLA Modules:
  0.0 195.9 jit_solution(5111954408993964318)
XLA Ops:
  6.5 0.7 fusion.33
  7.3 6.1 %gather_fusion.1 = s32[1024]{0:T(1024)S(1)} fusion(s32[2048]{0:T(1024)S(1)} %copy-done, s32[1024]{0:T(1024)S(1)} %get-tuple-element.20), kind=kCustom, calls=%fused_computation.5 | custom fusion | bytes 12288 | tf_op jit(solution)/shard_map/gather | solution.py:23
  13.4 0.7 copy-done.1
  14.1 6.1 %gather_fusion = s32[1024]{0:T(1024)S(1)} fusion(s32[2048]{0:T(1024)S(1)} %copy-done.1, s32[1024]{0:T(1024)S(1)} %get-tuple-element.20), kind=kCustom, calls=%fused_computation.4 | custom fusion | bytes 12288 | tf_op jit(solution)/shard_map/gather | solution.py:22
  20.3 0.1 copy.37
  20.4 2.8 %gather_fusion.14 = f32[1024,32]{1,0:T(8,128)S(1)} fusion(f32[32,256]{0,1:T(8,128)S(1)} %copy.37, s32[1024]{0:T(1024)S(1)} %fusion.34), kind=kCustom, calls=%fused_computation.clone | custom fusion | bytes 266240 | tf_op jit(solution)/shard_map/jit(_take)/gather | solution.py:23
  23.2 1.1 bitcast_select_fusion.1
  24.5 0.1 add.170
  24.5 0.5 copy-done.7
  25.1 0.1 add.184
  25.3 0.1 add.168
  25.4 0.5 copy-done.2
  25.9 6.1 %gather_fusion.4 = f32[1024]{0:T(1024)S(1)} fusion(f32[2048]{0:T(1024)S(1)} %copy-done.2, s32[1024]{0:T(1024)S(1)} %get-tuple-element.20), kind=kCustom, calls=%fused_computation.8 | custom fusion | bytes 12288 | tf_op jit(solution)/shard_map/gather | solution.py:44
  32.1 6.2 %gather_fusion.2 = f32[1024]{0:T(1024)S(1)} fusion(f32[2048]{0:T(1024)S(1)} %copy-done.3, s32[1024]{0:T(1024)S(1)} %get-tuple-element.20), kind=kCustom, calls=%fused_computation.6 | custom fusion | bytes 12288 | tf_op jit(solution)/shard_map/gather | solution.py:41
  38.3 27.2 %all-reduce.5.cloned.1.call-done = f32[32,1024]{0,1:T(8,128)} async-done(((f32[32,1024]{0,1:T(8,128)}), f32[32,1024]{0,1:T(8,128)}) %all-reduce.5.cloned.1.call-update) | async-done | bytes 131088 | tf_op jit(solution)/shard_map/psum | solution.py:24
  65.5 1.4 multiply_reduce_fusion.1
  67.0 13.2 %all-reduce.1 = (f32[1024]{0:T(1024)S(1)}, f32[1024]{0:T(1024)S(1)}) all-reduce(f32[1024]{0:T(1024)S(1)} %get-tuple-element.10, f32[1024]{0:T(1024)S(1)} %get-tuple-element.9), channel_id=1, replica_groups=mesh['region'=4,'member'=8] {'member'}, use_global_device_ids=true, to_apply=%region_2.4 | all-reduce | flops 2048 | bytes 16384 | tf_op jit(solution)/shard_map/psum | solution.py:31
  80.2 0.2 broadcast_subtract_fusion.1
  80.4 0.7 gather_fusion.15
  81.2 1.1 fusion.13
  82.5 6.1 %gather_fusion.8 = s32[1024]{0:T(1024)S(1)} fusion(s32[2048]{0:T(1024)S(1)} %copy-done, s32[1024]{0:T(1024)S(1)} %get-tuple-element.19), kind=kCustom, calls=%fused_computation.12 | custom fusion | bytes 12288 | tf_op jit(solution)/shard_map/gather | solution.py:23
  88.6 6.2 %gather_fusion.7 = s32[1024]{0:T(1024)S(1)} fusion(s32[2048]{0:T(1024)S(1)} %copy-done.1, s32[1024]{0:T(1024)S(1)} %get-tuple-element.19), kind=kCustom, calls=%fused_computation.11 | custom fusion | bytes 12288 | tf_op jit(solution)/shard_map/gather | solution.py:22
  94.8 1.4 gather_fusion.6
  96.2 1.4 gather_fusion.3
  97.6 1.4 gather_fusion.5
  99.0 5.0 %all-gather.5.cloned.1.call-done = f32[16,128,128]{2,1,0:T(8,128)} async-done(((f32[2,128,128]{2,1,0:T(8,128)}), f32[16,128,128]{2,1,0:T(8,128)}) %all-gather.5.cloned.1.call-update) | async-done | bytes 1048592 | tf_op jit(solution)/shard_map/all_gather | solution.py:38
  103.9 1.3 reduce_sum.55
  105.2 0.3 convolution_bitcast_fusion.1
  105.5 0.3 fusion.4
  105.9 0.1 copy.41
  106.0 2.8 %gather_fusion.16 = f32[1024,32]{1,0:T(8,128)S(1)} fusion(f32[32,256]{0,1:T(8,128)S(1)} %copy.41, s32[1024]{0:T(1024)S(1)} %fusion.35), kind=kCustom, calls=%fused_computation.2.clone | custom fusion | bytes 266240 | tf_op jit(solution)/shard_map/jit(_take)/gather | solution.py:23
  108.8 1.1 bitcast_select_fusion
  110.0 6.2 %gather_fusion.11 = f32[1024]{0:T(1024)S(1)} fusion(f32[2048]{0:T(1024)S(1)} %copy-done.2, s32[1024]{0:T(1024)S(1)} %get-tuple-element.19), kind=kCustom, calls=%fused_computation.15 | custom fusion | bytes 12288 | tf_op jit(solution)/shard_map/gather | solution.py:44
  116.2 6.2 %gather_fusion.9 = f32[1024]{0:T(1024)S(1)} fusion(f32[2048]{0:T(1024)S(1)} %copy-done.3, s32[1024]{0:T(1024)S(1)} %get-tuple-element.19), kind=kCustom, calls=%fused_computation.13 | custom fusion | bytes 12288 | tf_op jit(solution)/shard_map/gather | solution.py:41
  122.3 26.0 %all-reduce.7.cloned.1.call-done = f32[32,1024]{0,1:T(8,128)} async-done(((f32[32,1024]{0,1:T(8,128)}), f32[32,1024]{0,1:T(8,128)}) %all-reduce.7.cloned.1.call-update) | async-done | bytes 131088 | tf_op jit(solution)/shard_map/psum | solution.py:24
  148.4 1.4 multiply_reduce_fusion
  149.8 13.2 %all-reduce = (f32[1024]{0:T(1024)S(1)}, f32[1024]{0:T(1024)S(1)}) all-reduce(f32[1024]{0:T(1024)S(1)} %get-tuple-element.8, f32[1024]{0:T(1024)S(1)} %get-tuple-element.6), channel_id=1, replica_groups=mesh['region'=4,'member'=8] {'member'}, use_global_device_ids=true, to_apply=%region_8.11 | all-reduce | flops 2048 | bytes 16384 | tf_op jit(solution)/shard_map/psum | solution.py:31
  163.1 0.2 broadcast_subtract_fusion
  163.3 0.7 gather_fusion.17
  164.1 1.1 fusion.10
  165.1 1.4 gather_fusion.13
  166.5 1.4 gather_fusion.10
  167.9 1.4 gather_fusion.12
  169.3 17.6 %all-gather.7.cloned.1.call-done = f32[16,128,128]{2,1,0:T(8,128)} async-done(((f32[2,128,128]{2,1,0:T(8,128)}), f32[16,128,128]{2,1,0:T(8,128)}) %all-gather.7.cloned.1.call-update) | async-done | bytes 1048592 | tf_op jit(solution)/shard_map/all_gather | solution.py:38
  186.8 1.3 reduce_sum.58
  188.1 0.3 convolution_bitcast_fusion
  188.4 0.3 fusion.1
  188.7 0.6 bitcast_subtract_fusion
  (44 shorter events, 0.8 us)
Async XLA Ops:
  6.5 0.7 copy-start
  6.5 59.0 %all-reduce.5.cloned.1.call-start = ((), (), s32[]{:S(2)}) async-start(), calls=%async_computation | async-start | bytes 1048576 | tf_op jit(solution)/shard_map/psum | solution.py:24
  13.4 0.7 copy-start.1
  14.1 6.2 %copy-start.6 = (f32[32,256]{1,0:T(8,128)S(1)}, f32[32,256]{1,0:T(8,128)}, u32[]{:S(2)}) copy-start(f32[32,256]{1,0:T(8,128)} %param.11) | copy-start | bytes 98308
  24.4 0.7 copy-start.7
  24.4 79.5 %all-gather.5.cloned.1.call-start = ((), (), s32[]{:S(2)}) async-start(), calls=%async_computation.2 | async-start | bytes 1179648 | tf_op jit(solution)/shard_map/all_gather | solution.py:38
  25.2 0.7 copy-start.2
  25.9 6.2 %copy-start.3 = (f32[2048]{0:T(1024)S(1)}, f32[2048]{0:T(1024)}, u32[]{:S(2)}) copy-start(f32[2048]{0:T(1024)} %param.13) | copy-start | bytes 24580
  65.5 14.7 %copy-start.4 = (f32[32,1024]{0,1:T(8,128)S(1)}, f32[32,1024]{0,1:T(8,128)}, u32[]{:S(2)}) copy-start(f32[32,1024]{0,1:T(8,128)} %all-reduce.5.cloned.1.call-done) | copy-start | bytes 393220
  82.3 66.1 %all-reduce.7.cloned.1.call-start = ((), (), s32[]{:S(2)}) async-start(), calls=%async_computation.1 | async-start | bytes 1048576 | tf_op jit(solution)/shard_map/psum | solution.py:24
  110.0 76.9 %all-gather.7.cloned.1.call-start = ((), (), s32[]{:S(2)}) async-start(), calls=%async_computation.3 | async-start | bytes 1179648 | tf_op jit(solution)/shard_map/all_gather | solution.py:38
  148.4 14.7 %copy-start.5 = (f32[32,1024]{0,1:T(8,128)S(1)}, f32[32,1024]{0,1:T(8,128)}, u32[]{:S(2)}) copy-start(f32[32,1024]{0,1:T(8,128)} %all-reduce.7.cloned.1.call-done) | copy-start | bytes 393220
Sparse Core Ops, SparseCore 0:
  24.5 40.9 all-reduce.4
  82.4 21.5 all-gather.4
  110.1 38.2 all-reduce.6
  165.3 21.5 all-gather.6
